TPU v7x, 256 devices: a whole 4x4x8 slice. The times are simulated.
256 devices in a mesh: sub: 64 (over x, z, core), col: 4 (over y).
Axes of the slice: x: 4, y: 4, z: 8, core: 2. Of those that a mesh axis runs over, the one named last changes fastest.
Arguments:
- flexibility: bfloat16 [64, 768, 768], P('sub')
- omega: bfloat16 [256, 24576], P('col', 'sub'), may hold values from -6 to 6
- block_row: int32 [64, 6], replicated, may hold values from 0 to 191, as said below
- block_sign: int32 [64, 6], replicated, may hold values from -1 to 1, as said below
Outputs:
- sketch: float32 [256, 24576], P('col', 'sub')
- basis: float32 [256, 24576], P('col', 'sub')
- factor: float32 [256, 256], replicated
Inputs may be any that keep to these rules, and one draw needn't show every extreme that they name: `block_row`: each row block is named by exactly two entries, one whose block_sign is 1 and one whose block_sign is -1. Row block b lies in the sketch columns of sub index b // 3. For any two sub indices p and q, the blocks of p's one substructure name row blocks of q either exactly 2 times or never. `block_sign`: every entry is -1 or 1.
All inputs are finite; a program needn't handle non-finite values.
Results may differ from a plain program's by a relative error of at most 0.0003.
Values may be sent and summed in bfloat16 or wider, within the bound.
A program may use at most 64 MiB of HBM per device.

v0:
```python
import jax
import jax.numpy as jnp
from jax import lax
from jax.sharding import PartitionSpec as P


def rank_within(owners):
    count = owners.shape[-1]
    same = owners[..., :, None] == owners[..., None, :]
    index = jnp.arange(count)
    earlier = index[None, :] < index[:, None]
    return jnp.sum(same & earlier, axis=-1)


def upper_factor(gram):
    order = gram.shape[0]
    index = jnp.arange(order)

    def eliminate(column, state):
        remain, upper = state
        row = lax.dynamic_index_in_dim(remain, column, 0, keepdims=False)
        pivot = jnp.sqrt(lax.dynamic_index_in_dim(row, column, 0, keepdims=False))
        scaled = jnp.where(index >= column, row / pivot, jnp.zeros_like(row))
        upper = lax.dynamic_update_slice_in_dim(upper, scaled[None, :], column, 0)
        remain = remain - scaled[:, None] * scaled[None, :]
        return (remain, upper)

    start = (gram, jnp.zeros_like(gram))
    ignored, upper = lax.fori_loop(0, order, eliminate, start)
    return upper


def upper_inverse(upper):
    order = upper.shape[0]
    index = jnp.arange(order)

    def substitute(turn, inverse):
        column = order - 1 - turn
        row = lax.dynamic_index_in_dim(upper, column, 0, keepdims=False)
        pivot = lax.dynamic_index_in_dim(row, column, 0, keepdims=False)
        unit = (index == column).astype(jnp.float32)
        known = jnp.dot(row, inverse, precision=lax.Precision.HIGHEST)
        solved = (unit - known) / pivot
        return lax.dynamic_update_slice_in_dim(inverse, solved[None, :], column, 0)

    return lax.fori_loop(0, order, substitute, jnp.zeros_like(upper))


def shards(flexibility, omega, block_row, block_sign):
    sub_count = lax.axis_size("sub")
    position = lax.axis_index("sub")
    sub_local = flexibility.shape[0]
    local_dofs = flexibility.shape[1]
    local_blocks = block_row.shape[1]
    block_len = local_dofs // local_blocks
    col_width = omega.shape[0]
    row_count = omega.shape[1]
    owned_blocks = row_count // block_len
    ref_count = sub_local * local_blocks
    capacity = max(2, (ref_count + sub_count - 1) // sub_count)
    slot_count = sub_count * capacity
    all_owner = block_row // owned_blocks
    all_rank = rank_within(all_owner)
    my_signs = lax.dynamic_index_in_dim(block_sign, position, 0, keepdims=False)
    my_slot = lax.dynamic_index_in_dim(all_owner * capacity + all_rank, position, 0, keepdims=False)
    hits = (all_owner == position)[:, None, :] & (
        all_rank[:, None, :] == jnp.arange(capacity)[None, :, None]
    )
    served = jnp.any(hits, axis=-1).reshape(slot_count)
    source_block = jnp.sum(
        jnp.where(hits, (block_row % owned_blocks)[:, None, :], 0), axis=-1
    ).reshape(slot_count)
    blocks = omega.reshape(col_width, owned_blocks, block_len)
    outgoing = jnp.take(blocks, source_block, axis=1).reshape(
        col_width, sub_count, capacity * block_len
    )
    incoming = lax.all_to_all(outgoing, "sub", split_axis=1, concat_axis=1, tiled=True)
    pieces = jnp.take(incoming.reshape(col_width, slot_count, block_len), my_slot, axis=1)
    signed = pieces * my_signs.astype(jnp.bfloat16)[None, :, None]
    response = jnp.einsum(
        "ksj,sij->ksi",
        signed.reshape(col_width, sub_local, local_dofs),
        flexibility,
        preferred_element_type=jnp.float32,
    )
    contrib = response.reshape(col_width, ref_count, block_len)
    route = (my_slot[:, None] == jnp.arange(slot_count)[None, :]).astype(
        jnp.float32
    ) * my_signs.astype(jnp.float32)[:, None]
    outgoing_back = jnp.einsum("krb,rq->kqb", contrib, route, precision=lax.Precision.HIGHEST)
    outgoing_back = outgoing_back.reshape(col_width, sub_count, capacity * block_len)
    returned = lax.all_to_all(outgoing_back, "sub", split_axis=1, concat_axis=1, tiled=True)
    collect = (
        (source_block[:, None] == jnp.arange(owned_blocks)[None, :]) & served[:, None]
    ).astype(jnp.float32)
    sketch = jnp.einsum(
        "kqb,qi->kib",
        returned.reshape(col_width, slot_count, block_len),
        collect,
        precision=lax.Precision.HIGHEST,
    )
    sketch = sketch.reshape(col_width, row_count)
    full = lax.all_gather(sketch, "col", axis=0, tiled=True)
    rows_total = row_count * sub_count
    local_gram = (
        lax.dot_general(full, full, (((1,), (1,)), ((), ())), precision=lax.Precision.HIGHEST)
        / rows_total
    )
    gram = lax.psum(local_gram, "sub")
    upper = upper_factor(gram)
    inverse = upper_inverse(upper)
    column_part = lax.dynamic_slice_in_dim(inverse, lax.axis_index("col") * col_width, col_width, 1)
    basis = lax.dot_general(
        column_part, full, (((0,), (0,)), ((), ())), precision=lax.Precision.HIGHEST
    )
    return (sketch, basis, upper)


def solution(mesh):
    placed = (P("sub", None, None), P("col", "sub"), P(), P())
    return jax.shard_map(
        shards,
        mesh=mesh,
        in_specs=placed,
        out_specs=(P("col", "sub"), P("col", "sub"), P()),
        check_vma=False,
    )
```

profile of v0, /device:TPU:1, one launch (start us, length us, event | category | flops | bytes accessed | tf_op | source)
XLA Modules:
  0.0 1963.2 jit_solution(2266155646979882207)
XLA Ops:
  10.8 2.7 copy.60
  13.6 2.7 gather.11
  16.7 2.5 copy.61
  19.3 13.1 all-to-all-start
  33.0 50.6 %all-to-all-done = bf16[64,64,256]{2,0,1:T(8,128)(2,1)S(1)} async-done(((bf16[64,64,256]{2,0,1:T(8,128)(2,1)}), bf16[64,64,256]{2,0,1:T(8,128)(2,1)S(1)}, u32[]{:S(2)}, u32[]{:S(2)}) %all-to-all-start) | async-done | bytes 2097184 | tf_op jit(solution)/shard_map/all_to_all | solution.py:77
  83.6 2.5 copy.62
  86.2 2.7 reshape.238
  88.8 2.7 copy.63
  91.5 2.2 gather_fusion.1
  94.3 5.2 convolution_bitcast_fusion
  99.5 5.2 reshape.241
  104.7 6.6 copy.65
  111.3 6.0 all-to-all-start.1
  118.0 95.2 %all-to-all-done.1 = f32[64,64,256]{2,0,1:T(8,128)} async-done(((f32[64,64,256]{2,0,1:T(8,128)}), f32[64,64,256]{2,0,1:T(8,128)}, u32[]{:S(2)}, u32[]{:S(2)}) %all-to-all-start.1) | async-done | bytes 4194336 | tf_op jit(solution)/shard_map/all_to_all | solution.py:92
  213.2 6.6 copy.66
  219.8 4.7 reshape.242
  224.5 3.6 fusion.30
  228.1 10.8 all_gather.3
  240.3 174.1 %all-reduce.2.cloned.1.call-done = f32[256,256]{1,0:T(8,128)} async-done(((f32[256,256]{1,0:T(8,128)}), f32[256,256]{1,0:T(8,128)}) %all-reduce.2.cloned.1.call-update) | async-done | bytes 262160 | tf_op jit(solution)/shard_map/psum | solution.py:109
  414.4 1146.5 %while.36 = (s32[]{:T(128)}, f32[256,256]{1,0:T(8,128)}, f32[256,256]{1,0:T(8,128)S(1)}, s32[]{:T(128)}, s32[]{:T(128)}, /*index=5*/s32[]{:T(128)}) while((s32[]{:T(128)}, f32[256,256]{1,0:T(8,128)}, f32[256,256]{1,0:T(8,128)S(1)}, s32[]{:T(128)}, s32[]{:T(128)}, /*index=5*/s32[]{:T(128)}) %tuple.87), condition=%wide.region_5.6_spmd.clone, body=%wide.region_4.5_spmd.clone.sunk | while | flops 132355 | bytes 534141 | solution.py:29
  421.6 1.7 multiply_subtract_fusion.2
  439.5 1.7 multiply_subtract_fusion.2
  466.4 1.7 multiply_subtract_fusion.2
  488.8 1.7 multiply_subtract_fusion.2
  533.5 1.7 multiply_subtract_fusion.2
  542.5 1.7 multiply_subtract_fusion.2
  551.5 1.7 multiply_subtract_fusion.2
  587.2 1.7 multiply_subtract_fusion.2
  681.3 1.7 multiply_subtract_fusion.2
  690.3 1.7 multiply_subtract_fusion.2
  699.2 1.7 multiply_subtract_fusion.2
  748.5 1.7 multiply_subtract_fusion.2
  784.3 1.7 multiply_subtract_fusion.2
  811.2 1.7 multiply_subtract_fusion.2
  847.0 1.7 multiply_subtract_fusion.2
  963.5 1.7 multiply_subtract_fusion.2
  999.3 1.7 multiply_subtract_fusion.2
  1017.2 1.7 multiply_subtract_fusion.2
  1075.5 1.7 multiply_subtract_fusion.2
  1080.0 1.7 multiply_subtract_fusion.2
  1084.5 1.7 multiply_subtract_fusion.2
  1097.9 1.7 multiply_subtract_fusion.2
  1156.1 1.7 multiply_subtract_fusion.2
  1178.5 1.7 multiply_subtract_fusion.2
  1196.4 1.7 multiply_subtract_fusion.2
  1236.7 1.7 multiply_subtract_fusion.2
  1245.7 1.7 multiply_subtract_fusion.2
  1561.0 394.2 %while.37 = (s32[]{:T(128)}, f32[256,256]{1,0:T(8,128)S(1)}, f32[256,256]{1,0:T(8,128)S(1)}, s32[]{:T(128)}, s32[]{:T(128)}, /*index=5*/s32[]{:T(128)}, s32[]{:T(128)}) while((s32[]{:T(128)}, f32[256,256]{1,0:T(8,128)S(1)}, f32[256,256]{1,0:T(8,128)S(1)}, s32[]{:T(128)}, s32[]{:T(128)}, /*index=5*/s32[]{:T(128)}, s32[]{:T(128)}) %tuple.90), condition=%wide.region_7.8_spmd.clone, body=%wide.region_6.7_spmd.clone.sunk | while | flops 787463 | bytes 268455 | solution.py:46
  (2577 shorter events, 1309.0 us)
Async XLA Ops:
  7.2 86.5 %copy-start = (bf16[1,768,768]{2,1,0:T(8,128)(2,1)S(1)}, bf16[1,768,768]{2,1,0:T(8,128)(2,1)}, u32[]{:S(2)}) copy-start(bf16[1,768,768]{2,1,0:T(8,128)(2,1)} %param.8) | copy-start | bytes 3538948
  19.3 13.1 copy-start.3
  19.3 64.4 %all-to-all-start = ((bf16[64,64,256]{2,0,1:T(8,128)(2,1)}), bf16[64,64,256]{2,0,1:T(8,128)(2,1)S(1)}, u32[]{:S(2)}, u32[]{:S(2)}) async-start(bf16[64,64,256]{2,0,1:T(8,128)(2,1)} %copy.61), calls=%async_computation | async-start | bytes 4194304 | tf_op jit(solution)/shard_map/all_to_all | solution.py:77
  111.3 101.9 %all-to-all-start.1 = ((f32[64,64,256]{2,0,1:T(8,128)}), f32[64,64,256]{2,0,1:T(8,128)}, u32[]{:S(2)}, u32[]{:S(2)}) async-start(f32[64,64,256]{2,0,1:T(8,128)} %copy.65), calls=%async_computation.1 | async-start | bytes 8388608 | tf_op jit(solution)/shard_map/all_to_all | solution.py:92
  117.3 297.1 %all-reduce.2.cloned.1.call-start = ((), (), s32[]{:S(2)}) async-start(), calls=%async_computation.2 | async-start | bytes 524288 | tf_op jit(solution)/shard_map/psum | solution.py:109
  228.1 186.3 %copy-start.1 = (f32[8,8,3,128]{3,1,2,0:T(8,128)}, f32[8,8,3,128]{3,1,2,0:T(8,128)S(1)}, u32[]{:S(2)}) copy-start(f32[8,8,3,128]{3,1,2,0:T(8,128)S(1)} %copy.79) | copy-start | bytes 294916
  1955.2 1.1 copy-start.2
Sparse Core Ops, SparseCore 0:
  240.4 173.8 all-reduce.1
where the time goes:
time: 2000 us; the launch traced here: 1960 us
  other arithmetic  800 us (40%)
  local copies, waits for them, and re-layouts  547 us (27%)
  waiting for transfers between devices  320 us (16%)
  loops' own time  193 us (10%)
  matrix products  59.1 us (3%)
    sub x256, other arithmetic, eliminate(): remain = remain - scaled[:, None] * scaled[None, :]  447 us
    dynamic_slice x256, local copies, waits for them, and re-layouts, eliminate(): pivot = jnp.sqrt(lax.dynamic_index_in_dim(row, column, 0, keepdims=False))  325 us
    another operation x1, loops' own time, upper_factor(): ignored, upper = lax.fori_loop(0, order, eliminate, start)  184 us
    select_n x512, other arithmetic, eliminate(): scaled = jnp.where(index >= column, row / pivot, jnp.zeros_like(row))  183 us
    psum x1, waiting for transfers between devices, shards(): gram = lax.psum(local_gram, 'sub')  174 us
    div x256, other arithmetic, substitute(): solved = (unit - known) / pivot  166 us
    dynamic_slice x256, local copies, waits for them, and re-layouts, substitute(): pivot = lax.dynamic_index_in_dim(row, column, 0, keepdims=False)  161 us
    all_to_all x1, waiting for transfers between devices, shards(): lax.all_to_all(outgoing_back, 'sub', split_axis=1, concat_axis=1, tiled=T...  95.2 us
  transfers between devices with their start and end apart: 3, of which 3 were waited for; matrix products, arithmetic and copies ran while one was open for 0% of the time, Pallas kernels for 0%

commit v1 on v0

v1 whole, which is shorter than its diff:
```python
import functools

import jax
import jax.numpy as jnp
from jax import lax
from jax.experimental import pallas as pl
from jax.experimental.pallas import tpu as pltpu
from jax.sharding import PartitionSpec as P

F32 = jnp.float32
BF16 = jnp.bfloat16
NN = (((1,), (0,)), ((), ()))
NT = (((1,), (1,)), ((), ()))


def mm1(a, b, dims=NN):
    return lax.dot_general(a.astype(BF16), b.astype(BF16), dims, preferred_element_type=F32)


def halves(a):
    high = a.astype(BF16)
    return high, (a - high.astype(F32)).astype(BF16)


def mm3(a, b, dims=NN):
    ah, al = halves(a)
    bh, bl = halves(b)
    dot = functools.partial(lax.dot_general, dimension_numbers=dims, preferred_element_type=F32)
    return dot(ah, bh) + (dot(ah, bl) + dot(al, bh))


def finish_kernel(full_ref, gram_ref, basis_ref, upper_ref, work, lower):
    order = gram_ref.shape[0]
    rows = basis_ref.shape[0]
    i_row = lax.broadcasted_iota(jnp.int32, (order, order), 0)
    i_col = lax.broadcasted_iota(jnp.int32, (order, order), 1)
    eye = jnp.where(i_row == i_col, 1.0, 0.0).astype(F32)
    phi_mask = jnp.where(i_row > i_col, 1.0, 0.5 * eye).astype(F32)
    gram = gram_ref[...]
    on_diag = gram * eye
    d_row = jnp.sum(on_diag, axis=0, keepdims=True)
    d_col = jnp.sum(on_diag, axis=1, keepdims=True)
    s_row = lax.rsqrt(d_row)
    s_col = lax.rsqrt(d_col)
    err = jnp.where(i_row == i_col, 0.0, gram * s_row * s_col)
    p = err * phi_mask
    n = mm1(p, p, NT) * phi_mask + mm1(p, p) - p
    z = err + n + mm1(n, err)
    resid = z + n.T + mm1(z, n, NT)
    p = resid * phi_mask
    n = n - p - mm1(p, n)
    z = err + n + mm3(n, err)
    resid = z + n.T + mm3(z, n, NT)
    p = resid * phi_mask
    n = n - p - mm1(p, n)
    miss = jnp.sum(resid * resid)
    z = err + n + mm3(n, err)
    upper_ref[...] = jnp.where(i_row <= i_col, (eye + z) * (d_row * s_row), 0.0)
    lower[...] = jnp.where(i_row >= i_col, (eye + n) * s_row, 0.0)

    @pl.when(jnp.logical_not(miss < 4e-6))
    def eliminate():
        work[...] = gram
        lower[...] = eye
        lane = lax.broadcasted_iota(jnp.int32, (1, order), 1)
        sub = lax.broadcasted_iota(jnp.int32, (order, 1), 0)

        @pl.loop(0, order)
        def step(j):
            remain = work[...]
            row = work[pl.ds(j, 1), :]
            pivot = jnp.sum(jnp.where(lane == j, row, 0.0), axis=1, keepdims=True)
            scale = 1.0 / jnp.sqrt(pivot)
            u_row = jnp.where(lane >= j, row * scale, 0.0)
            column = jnp.sum(jnp.where(i_col == j, remain, 0.0), axis=1, keepdims=True)
            column = jnp.where(sub > j, column * scale, 0.0)
            l_row = lower[pl.ds(j, 1), :] * scale
            upper_ref[pl.ds(j, 1), :] = u_row
            work[...] = remain - column * u_row
            below = lower[...] - column * l_row
            lower[...] = jnp.where(sub == j, l_row, below)

    mine = pl.ds(pl.multiple_of(lax.axis_index("col") * rows, rows), rows)
    basis_ref[...] = mm3(lower[mine, :], full_ref[...])


def finish(full, gram, rows):
    order, width = full.shape
    return pl.pallas_call(
        finish_kernel,
        out_shape=(
            jax.ShapeDtypeStruct((rows, width), F32),
            jax.ShapeDtypeStruct((order, order), F32),
        ),
        in_specs=[pl.BlockSpec(memory_space=pltpu.VMEM)] * 2,
        out_specs=(pl.BlockSpec(memory_space=pltpu.VMEM),) * 2,
        scratch_shapes=[pltpu.VMEM((order, order), F32)] * 2,
        name="factor_and_basis",
    )(full, gram)


def exchange(x):
    return lax.all_to_all(x, "sub", split_axis=0, concat_axis=0, tiled=True)


def shards(flexibility, omega, block_row, block_sign):
    sub_count = lax.axis_size("sub")
    position = lax.axis_index("sub")
    local_dofs = flexibility.shape[1]
    local_blocks = block_row.shape[1]
    block_len = local_dofs // local_blocks
    col_width, row_count = omega.shape
    owned = row_count // block_len
    blocks = sub_count * owned
    refs = sub_count * local_blocks
    pick = block_row.reshape(refs, 1) == jnp.arange(blocks)[None, :]
    pick = pick.astype(F32) * block_sign.reshape(refs, 1).astype(F32)
    row_omega = exchange(omega).reshape(blocks, block_len)
    wanted = jnp.dot(pick.astype(BF16), row_omega, preferred_element_type=F32).astype(BF16)
    signed = exchange(wanted.reshape(sub_count, local_dofs))
    response = lax.dot_general(signed, flexibility[0], NT, preferred_element_type=F32)
    contrib = exchange(response).reshape(refs, block_len)
    total = lax.dot_general(pick, contrib, (((0,), (0,)), ((), ())), precision=lax.Precision.HIGHEST)
    sketch = exchange(total.reshape(sub_count, row_count))
    full = lax.all_gather(sketch, "col", axis=0, tiled=True)
    part = lax.dot_general(sketch, full, NT, precision=lax.Precision.HIGHEST) / (row_count * sub_count)
    mine = jnp.sum(exchange(part), axis=0, keepdims=True)
    gram = lax.all_gather(lax.all_gather(mine, "sub", axis=0, tiled=True), "col", axis=0, tiled=True)
    basis, upper = finish(full, gram, col_width)
    return (sketch, basis, upper)


def solution(mesh):
    placed = (P("sub", None, None), P("col", "sub"), P(), P())
    return jax.shard_map(
        shards,
        mesh=mesh,
        in_specs=placed,
        out_specs=(P("col", "sub"), P("col", "sub"), P()),
        check_vma=False,
    )
```

time: 2000 us -> 204 us (0.10); the launches traced: 1960 us -> 202 us
  other arithmetic: 800 us -> 3.72 us
  local copies, waits for them, and re-layouts: 547 us -> 3.03 us
  waiting for transfers between devices: 320 us -> 7.94 us
  loops' own time: 193 us -> 0 us
  blocking collectives: 10.8 us -> 124 us
  matrix products: 59.1 us -> 2.16 us
  Pallas kernels: 0 us -> 47.3 us
    dynamic_slice x513 -> x0, local copies, waits for them, and re-layouts: 486 us -> none  [the longest x256 325 us: eliminate(): pivot = jnp.sqrt(lax.dynamic_index_in_dim(row, column, 0, keepdims=False))]
    sub x256 -> x0, other arithmetic: 447 us -> none  [eliminate(): remain = remain - scaled[:, None] * scaled[None, :]]
    another operation x2 -> x0, loops' own time: 193 us -> none  [the longest x1 184 us: upper_factor(): ignored, upper = lax.fori_loop(0, order, eliminate, start)]
    select_n x516 -> x0, other arithmetic: 184 us -> none  [the longest x512 183 us: eliminate(): scaled = jnp.where(index >= column, row / pivot, jnp.zeros_like(row))]
    psum x1 -> x0, waiting for transfers between devices: 174 us -> none  [shards(): gram = lax.psum(local_gram, 'sub')]
    div x256 -> x0, other arithmetic: 166 us -> none  [substitute(): solved = (unit - known) / pivot]
    all_to_all x2 -> x1, waiting for transfers between devices: 146 us -> 7.94 us  [exchange(): return lax.all_to_all(x, 'sub', split_axis=0, concat_axis=0, tiled=True)]
    all_to_all x0 -> x4, blocking collectives: none -> 61 us  [exchange(): return lax.all_to_all(x, 'sub', split_axis=0, concat_axis=0, tiled=True)]
  transfers between devices with their start and end apart: 3 -> 1, of which waited for: 3 -> 1; matrix products, arithmetic and copies ran while one was open for 0% -> 1% of each run, Pallas kernels for 0% -> 0%
where the time goes in v1:
time: 204 us; the launch traced here: 202 us
  blocking collectives  124 us (61%)
  Pallas kernels  47.3 us (23%)
  starting transfers between devices  13 us (6%)
  waiting for transfers between devices  7.94 us (4%)
  other arithmetic  3.72 us (2%)
  local copies, waits for them, and re-layouts  3.03 us (1%)
  matrix products  2.16 us (1%)
    all_to_all x4, blocking collectives, exchange(): return lax.all_to_all(x, 'sub', split_axis=0, concat_axis=0, tiled=True)  61 us
    pallas_call x1, Pallas kernels, finish(): pl.pallas_call(finish_kernel, out_shape=(jax.ShapeDtypeStruct((rows, widt...  47.3 us
    all_gather x1, blocking collectives, shards(): lax.all_gather(mine, 'sub', axis=0, tiled=True)  41.7 us
    all_to_all x1, starting transfers between devices, exchange(): return lax.all_to_all(x, 'sub', split_axis=0, concat_axis=0, tiled=True)  13 us
    all_gather x1, blocking collectives, shards(): full = lax.all_gather(sketch, 'col', axis=0, tiled=True)  10.8 us
    all_gather x1, blocking collectives, shards(): lax.all_gather(lax.all_gather(mine, 'sub', axis=0, tiled=True), 'col', ax...  10.6 us
    all_to_all x1, waiting for transfers between devices, exchange(): return lax.all_to_all(x, 'sub', split_axis=0, concat_axis=0, tiled=True)  7.94 us
  transfers between devices with their start and end apart: 1, of which 1 were waited for; matrix products, arithmetic and copies ran while one was open for 1% of the time, Pallas kernels for 0%

profile of v1, /device:TPU:1, one launch (start us, length us, event | category | flops | bytes accessed | tf_op | source)
XLA Modules:
  0.0 202.1 jit_solution(2912550759962876724)
XLA Ops:
  0.6 0.0 copy-start
  0.6 0.5 broadcast.14
  1.2 1.5 reduce.2
  2.6 0.7 reshape.47
  3.4 13.0 %all-to-all-start = ((bf16[64,2,192]{2,1,0:T(2,128)(2,1)}), bf16[64,2,192]{2,1,0:T(2,128)(2,1)S(1)}, u32[]{:S(2)}, u32[]{:S(2)}) async-start(bf16[64,2,192]{2,1,0:T(2,128)(2,1)} %reshape.47), calls=%async_computation | async-start | bytes 131072 | tf_op jit(solution)/shard_map/all_to_all | solution.py:103
  16.3 0.7 convert_element_type.18
  17.0 0.1 copy.17
  17.1 0.1 convert_element_type.19
  17.3 0.8 copy.16
  18.1 0.1 eq.15
  18.2 7.9 %all-to-all-done = bf16[64,2,192]{2,1,0:T(2,128)(2,1)S(1)} async-done(((bf16[64,2,192]{2,1,0:T(2,128)(2,1)}), bf16[64,2,192]{2,1,0:T(2,128)(2,1)S(1)}, u32[]{:S(2)}, u32[]{:S(2)}) %all-to-all-start) | async-done | bytes 49184 | tf_op jit(solution)/shard_map/all_to_all | solution.py:103
  26.1 0.1 reshape.48
  26.3 0.3 reduce.1
  26.6 0.3 convolution_convert_fusion
  26.9 1.2 reduce.3
  28.2 14.0 %all_to_all.52 = bf16[64,2,384]{2,1,0:T(2,128)(2,1)S(1)} all-to-all(bf16[64,2,384]{2,1,0:T(2,128)(2,1)S(1)} %reshape.49), channel_id=1, replica_groups=mesh['sub'=64,'col'=4] {'sub'}, dimensions={0} | all-to-all | bytes 196608 | tf_op jit(solution)/shard_map/all_to_all | solution.py:103
  42.2 0.1 reshape.50
  42.3 0.0 copy-done
  42.3 0.5 fusion.2
  42.8 0.2 copy.20
  43.0 15.1 %all_to_all.53 = f32[64,1,768]{2,1,0:T(1,128)S(1)} all-to-all(f32[64,1,768]{2,1,0:T(1,128)S(1)} %copy.20), channel_id=1, replica_groups=mesh['sub'=64,'col'=4] {'sub'}, dimensions={0} | all-to-all | bytes 393216 | tf_op jit(solution)/shard_map/all_to_all | solution.py:103
  58.1 0.9 fusion.6
  59.0 15.7 %all_to_all.54 = f32[64,1,384]{2,1,0:T(1,128)S(1)} all-to-all(f32[64,1,384]{2,1,0:T(1,128)S(1)} %bitcast.32), channel_id=1, replica_groups=mesh['sub'=64,'col'=4] {'sub'}, dimensions={0} | all-to-all | bytes 196608 | tf_op jit(solution)/shard_map/all_to_all | solution.py:103
  74.7 0.0 copy-start.2
  74.7 10.8 %all-gather = f32[256,1,384]{2,0,1:T(8,128)S(1)} all-gather(f32[64,1,384]{2,0,1:T(8,128)S(1)} %copy.35), channel_id=2, replica_groups=mesh['sub'=64,'col'=4] {'col'}, dimensions={0}, use_global_device_ids=true | all-gather | bytes 491520 | tf_op jit(solution)/shard_map/all_gather | solution.py:125
  85.5 0.0 copy-start.1
  85.5 0.5 fusion.5
  86.0 0.1 copy.23
  86.1 16.2 %all_to_all.55 = f32[64,1,256]{2,1,0:T(1,128)S(1)} all-to-all(f32[64,1,256]{2,1,0:T(1,128)S(1)} %copy.23), channel_id=1, replica_groups=mesh['sub'=64,'col'=4] {'sub'}, dimensions={0} | all-to-all | bytes 131072 | tf_op jit(solution)/shard_map/all_to_all | solution.py:103
  102.3 0.1 reduce_sum.9
  102.4 41.7 %all-gather.2 = f32[64,1,256]{2,1,0:T(1,128)S(1)} all-gather(f32[1,1,256]{2,1,0:T(1,128)S(1)} %bitcast.34), channel_id=3, replica_groups=mesh['sub'=64,'col'=4] {'sub'}, dimensions={0}, use_global_device_ids=true | all-gather | bytes 66560 | tf_op jit(solution)/shard_map/all_gather | solution.py:128
  144.1 10.6 %all_gather.11.gram_ref = f32[256,256]{1,0:T(8,128)} all-gather(f32[64,256]{1,0:T(8,128)S(1)} %bitcast.30), channel_id=1, replica_groups=mesh['sub'=64,'col'=4] {'col'}, dimensions={0}, use_global_device_ids=true | all-gather | bytes 327680 | tf_op jit(solution)/shard_map/all_gather | solution.py:128
  154.7 0.0 copy-done.1
  154.8 47.3 %factor_and_basis.1 = (f32[64,384]{1,0:T(8,128)}, f32[256,256]{1,0:T(8,128)}) custom-call(f32[256,384]{1,0:T(8,128)} %bitcast.27, f32[256,256]{1,0:T(8,128)} %all_gather.11.gram_ref), custom_call_target="tpu_custom_call" | custom-call | tf_op jit(solution)/shard_map/factor_and_basis/pallas_call | solution.py:89
  202.1 0.0 copy-done.2
  (5 shorter events, 0.1 us)
Async XLA Ops:
  0.6 41.7 %copy-start = (bf16[1,768,768]{2,1,0:T(8,128)(2,1)S(1)}, bf16[1,768,768]{2,1,0:T(8,128)(2,1)}, u32[]{:S(2)}) copy-start(bf16[1,768,768]{2,1,0:T(8,128)(2,1)} %param.4) | copy-start | bytes 3538948
  3.4 22.8 %all-to-all-start = ((bf16[64,2,192]{2,1,0:T(2,128)(2,1)}), bf16[64,2,192]{2,1,0:T(2,128)(2,1)S(1)}, u32[]{:S(2)}, u32[]{:S(2)}) async-start(bf16[64,2,192]{2,1,0:T(2,128)(2,1)} %reshape.47), calls=%async_computation | async-start | bytes 131072 | tf_op jit(solution)/shard_map/all_to_all | solution.py:103
  74.7 127.4 %copy-start.2 = (f32[64,1,384]{2,0,1:T(8,128)}, f32[64,1,384]{2,0,1:T(8,128)S(1)}, u32[]{:S(2)}) copy-start(f32[64,1,384]{2,0,1:T(8,128)S(1)} %copy.35) | copy-start | bytes 294916
  85.5 69.2 %copy-start.1 = (f32[256,1,384]{2,0,1:T(8,128)}, f32[256,1,384]{2,0,1:T(8,128)S(1)}, u32[]{:S(2)}) copy-start(f32[256,1,384]{2,0,1:T(8,128)S(1)} %all-gather) | copy-start | bytes 1179652

commit v2 on v1

--- a/solution.py
+++ b/solution.py
@@ -29,7 +29,7 @@
     return dot(ah, bh) + (dot(ah, bl) + dot(al, bh))
 
 
-def finish_kernel(full_ref, gram_ref, basis_ref, upper_ref, work, lower):
+def finish_kernel(full_ref, gram_ref, sketch_ref, basis_ref, upper_ref, work, lower):
     order = gram_ref.shape[0]
     rows = basis_ref.shape[0]
     i_row = lax.broadcasted_iota(jnp.int32, (order, order), 0)
@@ -82,6 +82,7 @@
 
     mine = pl.ds(pl.multiple_of(lax.axis_index("col") * rows, rows), rows)
     basis_ref[...] = mm3(lower[mine, :], full_ref[...])
+    sketch_ref[...] = full_ref[mine, :]
 
 
 def finish(full, gram, rows):
@@ -90,44 +91,191 @@
         finish_kernel,
         out_shape=(
             jax.ShapeDtypeStruct((rows, width), F32),
+            jax.ShapeDtypeStruct((rows, width), F32),
             jax.ShapeDtypeStruct((order, order), F32),
         ),
         in_specs=[pl.BlockSpec(memory_space=pltpu.VMEM)] * 2,
-        out_specs=(pl.BlockSpec(memory_space=pltpu.VMEM),) * 2,
+        out_specs=(pl.BlockSpec(memory_space=pltpu.VMEM),) * 3,
         scratch_shapes=[pltpu.VMEM((order, order), F32)] * 2,
         name="factor_and_basis",
     )(full, gram)
 
 
-def exchange(x):
-    return lax.all_to_all(x, "sub", split_axis=0, concat_axis=0, tiled=True)
+MESH = pl.DeviceIdType.MESH
+TN = (((0,), (0,)), ((), ()))
+
+
+def stack_lanes(x, length):
+    return jnp.concatenate([x[:, k : k + length] for k in range(0, x.shape[1], length)], axis=0)
+
+
+def spread_rows(x, parts):
+    length = x.shape[0] // parts
+    return jnp.concatenate([x[k * length : (k + 1) * length] for k in range(parts)], axis=1)
+
+
+def sketch_kernel(
+    n, m, omega_ref, flex_ref, row_ref, sign_ref, full_ref, gram_ref,
+    spare, flex, a_src, a_dst, b_src, b_dst, c_src, c_dst, d_src, full, g_src, g_dst, h_src, gram,
+    flex_sem, send, recv,
+):
+    me = lax.axis_index("sub")
+    col = lax.axis_index("col")
+    rows, width = a_src.shape
+    refs = row_ref.shape[0]
+    length = b_src.shape[1] // refs
+    owned = width // length
+
+    load = pltpu.make_async_copy(flex_ref, flex, flex_sem)
+    load.start()
+
+    barrier = pltpu.get_barrier_semaphore()
+
+    def greet(k, carry):
+        pl.semaphore_signal(
+            barrier, inc=1, device_id={"sub": lax.rem(me + k, n)}, device_id_type=MESH
+        )
+        return carry
+
+    lax.fori_loop(1, n, greet, 0)
+    for k in range(1, m):
+        pl.semaphore_signal(
+            barrier, inc=1, device_id={"col": lax.rem(col + k, m)}, device_id_type=MESH
+        )
+    a_src[...] = omega_ref[...].astype(F32)
+    pl.semaphore_wait(barrier, n - 1 + m - 1)
+
+    def start(phase, source, target):
+        own = pltpu.make_async_copy(source(me), target, recv.at[phase])
+        own.start()
+        pltpu.make_async_copy(
+            source(me), spare.at[phase, :, pl.ds(0, target.shape[1])], send.at[phase]
+        ).start()
+
+        def put(k, carry):
+            peer = lax.rem(me + k, n)
+            pltpu.make_async_remote_copy(
+                src_ref=source(peer), dst_ref=target, send_sem=send.at[phase],
+                recv_sem=recv.at[phase], device_id={"sub": peer}, device_id_type=MESH,
+            ).start()
+            return carry
+
+        lax.fori_loop(1, n, put, 0)
+
+    def arrive(phase, whole):
+        pltpu.make_async_copy(whole, whole, recv.at[phase]).wait()
+
+    def start_col(phase, ref):
+        for k in range(1, m):
+            pltpu.make_async_remote_copy(
+                src_ref=ref.at[col], dst_ref=ref.at[col], send_sem=send.at[phase],
+                recv_sem=recv.at[phase], device_id={"col": lax.rem(col + k, m)},
+                device_id_type=MESH,
+            ).start()
+
+    def row_of(ref):
+        return lambda r: ref.at[pl.ds(r, 1), :]
+
+    start(0, row_of(a_src), a_dst.at[pl.ds(me, 1), :])
+    spot = lax.broadcasted_iota(jnp.int32, (owned * n, n), 0)
+    piece = sum([jnp.where(spot >= n * j, 1, 0) for j in range(1, owned)])
+    named = owned * (spot - n * piece) + piece
+    pick = jnp.concatenate(
+        [
+            jnp.where(row_ref[l : l + 1, :] == named, sign_ref[l : l + 1, :], 0).astype(F32)
+            for l in range(refs)
+        ],
+        axis=1,
+    ).astype(BF16)
+    arrive(0, a_dst)
+    wanted = lax.dot_general(
+        pick, stack_lanes(a_dst[...], length).astype(BF16), TN, preferred_element_type=F32
+    )
+    b_src[...] = spread_rows(wanted, refs)
+
+    start(1, row_of(b_src), b_dst.at[pl.ds(me, 1), :])
+    load.wait()
+    arrive(1, b_dst)
+    c_src[...] = lax.dot_general(
+        b_dst[...].astype(BF16), flex[...], NT, preferred_element_type=F32
+    )
+
+    start(2, row_of(c_src), c_dst.at[pl.ds(me, 1), :])
+    arrive(2, c_dst)
+    terms = stack_lanes(c_dst[...], length)
+    high, rest = halves(terms)
+    middle, low = halves(terms - high.astype(F32))
+    total = sum(
+        [lax.dot_general(pick, t, NN, preferred_element_type=F32) for t in (low, middle, high)]
+    )
+    d_src[...] = spread_rows(total, owned)
+
+    start(3, row_of(d_src), full.at[col, pl.ds(me, 1), :])
+    arrive(3, full.at[col])
+    start_col(4, full)
+    arrive(4, full.at[pl.ds(0, m - 1)])
+    whole = full[...].reshape(m * rows, width)
+    full_ref[...] = whole
+    g_src[...] = mm3(full[col], whole, NT)
+
+    start(5, row_of(g_src), g_dst.at[pl.ds(me, 1), :])
+    arrive(5, g_dst)
+    h_src[...] = jnp.sum(g_dst[...], axis=0, keepdims=True) / (width * n)
+
+    start(6, lambda r: h_src, gram.at[col, pl.ds(me, 1), :])
+    arrive(6, gram.at[col])
+    start_col(7, gram)
+    arrive(7, gram.at[pl.ds(0, m - 1)])
+    gram_ref[...] = gram[...].reshape(m * rows, m * rows)
+
+    for phase, ref in ((0, a_src), (1, b_src), (2, c_src), (3, d_src), (5, g_src), (6, g_dst)):
+        pltpu.make_async_copy(ref, ref, send.at[phase]).wait()
+    for phase, ref in ((4, full), (7, gram)):
+        sent = ref.at[pl.ds(0, m - 1)]
+        pltpu.make_async_copy(sent, sent, send.at[phase]).wait()
+
+
+def sketch_and_gram(omega, flexibility, block_row, block_sign):
+    n, m = lax.axis_size("sub"), lax.axis_size("col")
+    rows, width = omega.shape
+    dofs = flexibility.shape[0]
+    order = m * rows
+    vmem = pl.BlockSpec(memory_space=pltpu.VMEM)
+    return pl.pallas_call(
+        functools.partial(sketch_kernel, n, m),
+        out_shape=(
+            jax.ShapeDtypeStruct((order, width), F32),
+            jax.ShapeDtypeStruct((order, order), F32),
+        ),
+        in_specs=[vmem, pl.BlockSpec(memory_space=pl.ANY), vmem, vmem],
+        out_specs=(vmem, vmem),
+        scratch_shapes=[
+            pltpu.VMEM((8, 1, dofs), F32),
+            pltpu.VMEM((dofs, dofs), BF16),
+            pltpu.VMEM((rows, width), F32),
+            pltpu.VMEM((n, width), F32),
+            pltpu.VMEM((n, dofs), F32),
+            pltpu.VMEM((rows, dofs), F32),
+            pltpu.VMEM((rows, dofs), F32),
+            pltpu.VMEM((n, dofs), F32),
+            pltpu.VMEM((n, width), F32),
+            pltpu.VMEM((m, rows, width), F32),
+            pltpu.VMEM((rows, order), F32),
+            pltpu.VMEM((n, order), F32),
+            pltpu.VMEM((1, order), F32),
+            pltpu.VMEM((m, rows, order), F32),
+            pltpu.SemaphoreType.DMA,
+            pltpu.SemaphoreType.DMA((8,)),
+            pltpu.SemaphoreType.DMA((8,)),
+        ],
+        compiler_params=pltpu.CompilerParams(collective_id=0, has_side_effects=True),
+        name="sketch_and_gram",
+    )(omega, flexibility, block_row.T, block_sign.T)
 
 
 def shards(flexibility, omega, block_row, block_sign):
-    sub_count = lax.axis_size("sub")
-    position = lax.axis_index("sub")
-    local_dofs = flexibility.shape[1]
-    local_blocks = block_row.shape[1]
-    block_len = local_dofs // local_blocks
-    col_width, row_count = omega.shape
-    owned = row_count // block_len
-    blocks = sub_count * owned
-    refs = sub_count * local_blocks
-    pick = block_row.reshape(refs, 1) == jnp.arange(blocks)[None, :]
-    pick = pick.astype(F32) * block_sign.reshape(refs, 1).astype(F32)
-    row_omega = exchange(omega).reshape(blocks, block_len)
-    wanted = jnp.dot(pick.astype(BF16), row_omega, preferred_element_type=F32).astype(BF16)
-    signed = exchange(wanted.reshape(sub_count, local_dofs))
-    response = lax.dot_general(signed, flexibility[0], NT, preferred_element_type=F32)
-    contrib = exchange(response).reshape(refs, block_len)
-    total = lax.dot_general(pick, contrib, (((0,), (0,)), ((), ())), precision=lax.Precision.HIGHEST)
-    sketch = exchange(total.reshape(sub_count, row_count))
-    full = lax.all_gather(sketch, "col", axis=0, tiled=True)
-    part = lax.dot_general(sketch, full, NT, precision=lax.Precision.HIGHEST) / (row_count * sub_count)
-    mine = jnp.sum(exchange(part), axis=0, keepdims=True)
-    gram = lax.all_gather(lax.all_gather(mine, "sub", axis=0, tiled=True), "col", axis=0, tiled=True)
-    basis, upper = finish(full, gram, col_width)
-    return (sketch, basis, upper)
+    full, gram = sketch_and_gram(omega, flexibility[0], block_row, block_sign)
+    return finish(full, gram, omega.shape[0])
 
 
 def solution(mesh):

time: 204 us -> 118 us (0.58)
  blocking collectives: 124 us -> 0 us
  Pallas kernels: 47.3 us -> 117 us
  starting transfers between devices: 13 us -> 0 us
  waiting for transfers between devices: 7.94 us -> 0 us
  other arithmetic: 3.72 us -> 0 us
  local copies, waits for them, and re-layouts: 3.03 us -> 0 us
  matrix products: 2.16 us -> 0 us
    pallas_call x0 -> x1, Pallas kernels: none -> 69.3 us  [sketch_and_gram(): pl.pallas_call(functools.partial(sketch_kernel, n, m), out_shape=(jax.Sha...]
    all_gather x3 -> x0, blocking collectives: 63.2 us -> none  [the longest x1 41.7 us: shards(): lax.all_gather(mine, 'sub', axis=0, tiled=True)]
    all_to_all x4 -> x0, blocking collectives: 61 us -> none  [exchange(): return lax.all_to_all(x, 'sub', split_axis=0, concat_axis=0, tiled=True)]
    all_to_all x1 -> x0, starting transfers between devices: 13 us -> none  [exchange(): return lax.all_to_all(x, 'sub', split_axis=0, concat_axis=0, tiled=True)]
    all_to_all x1 -> x0, waiting for transfers between devices: 7.94 us -> none  [exchange(): return lax.all_to_all(x, 'sub', split_axis=0, concat_axis=0, tiled=True)]
    all_to_all x3 -> x0, other arithmetic: 2.93 us -> none  [exchange(): return lax.all_to_all(x, 'sub', split_axis=0, concat_axis=0, tiled=True)]
    dot_general x4 -> x0, matrix products: 2.16 us -> none  [the longest x1 0.91 us: shards(): lax.dot_general(pick, contrib, (((0,), (0,)), ((), ())), precision=lax.Pr...]
  transfers between devices with their start and end apart: 1 -> 0, of which waited for: 1 -> 0; matrix products, arithmetic and copies ran while one was open for 1% -> 0% of each run, Pallas kernels for 0% -> 0%
where the time goes in v2:
time: 118 us; the launch traced here: 117 us
  Pallas kernels  117 us (99%)
    pallas_call x1, Pallas kernels, sketch_and_gram(): pl.pallas_call(functools.partial(sketch_kernel, n, m), out_shape=(jax.Sha...  69.3 us
    pallas_call x1, Pallas kernels, finish(): pl.pallas_call(finish_kernel, out_shape=(jax.ShapeDtypeStruct((rows, widt...  47.4 us

profile of v2, /device:TPU:1, one launch (start us, length us, event | category | flops | bytes accessed | tf_op | source)
XLA Modules:
  0.0 117.4 jit_solution(14677530009869264454)
XLA Ops:
  0.6 69.3 %sketch_and_gram.1 = (f32[256,384]{1,0:T(8,128)}, f32[256,256]{1,0:T(8,128)}) custom-call(bf16[64,384]{1,0:T(8,128)(2,1)} %omega_ref.1, bf16[768,768]{1,0:T(8,128)(2,1)} %bitcast.3, s32[6,64]{1,0:T(8,128)} %bitcast.4, s32[6,64]{1,0:T(8,128)} %bitcast.5), custom_call_target="tpu_custom_call" | custom-call | tf_op jit(solution)/shard_map/sketch_and_gram/pallas_call | solution.py:244
  70.0 47.4 %factor_and_basis.1 = (f32[64,384]{1,0:T(8,128)}, f32[64,384]{1,0:T(8,128)}, f32[256,256]{1,0:T(8,128)}) custom-call(f32[256,384]{1,0:T(8,128)} %get-tuple-element.5.full_ref, f32[256,256]{1,0:T(8,128)} %get-tuple-element.6.gram_ref), custom_call_target="tpu_custom_call" | custom-call | tf_op jit(solution)/shard_map/factor_and_basis/pallas_call | solution.py:90

commit v3 on v2

--- a/solution.py
+++ b/solution.py
@@ -102,6 +102,8 @@
 
 
 MESH = pl.DeviceIdType.MESH
+RING = 8
+PAIR = 2
 TN = (((0,), (0,)), ((), ()))
 
 
@@ -114,9 +116,14 @@
     return jnp.concatenate([x[k * length : (k + 1) * length] for k in range(parts)], axis=1)
 
 
+def centre_out(i, size):
+    half = lax.div(i + 1, 2)
+    return size // 2 + half * (1 - 2 * lax.rem(i, 2))
+
+
 def sketch_kernel(
     n, m, omega_ref, flex_ref, row_ref, sign_ref, full_ref, gram_ref,
-    spare, flex, a_src, a_dst, b_src, b_dst, c_src, c_dst, d_src, full, g_src, g_dst, h_src, gram,
+    spare, flex, a_src, a_dst, b_src, b_dst, c_src, c_dst, d_src, full, g_src, g_dst, h_src, h_dst, i_src, gram,
     flex_sem, send, recv,
 ):
     me = lax.axis_index("sub")
@@ -129,21 +136,47 @@
     load = pltpu.make_async_copy(flex_ref, flex, flex_sem)
     load.start()
 
+    across = n // (RING * PAIR)
+    plane = across * PAIR
+    my_x = lax.div(me, RING * PAIR)
+    my_z = lax.rem(lax.div(me, PAIR), RING)
+    my_core = lax.rem(me, PAIR)
+    my_part = my_x * PAIR + my_core
+
+    def at(x, z, core):
+        x, z, core = lax.rem(x, across), lax.rem(z, RING), lax.rem(core, PAIR)
+        return (x * RING + z) * PAIR + core
+
+    def peer_of(k):
+        in_plane = lax.rem(k, plane)
+        dz = centre_out(lax.div(k, plane), RING)
+        dx = centre_out(lax.div(in_plane, PAIR), across)
+        return at(my_x + dx, my_z + dz, my_core + 1 - lax.rem(in_plane, PAIR))
+
+    plane_mates = [
+        (dy, dx, core)
+        for dy in (2, 1, 3, 0)
+        for dx in (2, 1, 3, 0)
+        for core in (1, 0)
+        if (dy, dx, core) != (0, 0, 0)
+    ]
     barrier = pltpu.get_barrier_semaphore()
 
     def greet(k, carry):
         pl.semaphore_signal(
-            barrier, inc=1, device_id={"sub": lax.rem(me + k, n)}, device_id_type=MESH
+            barrier, inc=1, device_id={"sub": peer_of(k)}, device_id_type=MESH
         )
         return carry
 
-    lax.fori_loop(1, n, greet, 0)
-    for k in range(1, m):
+    lax.fori_loop(0, n - 1, greet, 0)
+    others = [mate for mate in plane_mates if mate[0]]
+    for dy, dx, core in others:
         pl.semaphore_signal(
-            barrier, inc=1, device_id={"col": lax.rem(col + k, m)}, device_id_type=MESH
+            barrier, inc=1, device_id_type=MESH,
+            device_id={"sub": at(my_x + dx, my_z, my_core + core), "col": lax.rem(col + dy, m)},
         )
     a_src[...] = omega_ref[...].astype(F32)
-    pl.semaphore_wait(barrier, n - 1 + m - 1)
+    pl.semaphore_wait(barrier, n - 1 + len(others))
 
     def start(phase, source, target):
         own = pltpu.make_async_copy(source(me), target, recv.at[phase])
@@ -153,14 +186,14 @@
         ).start()
 
         def put(k, carry):
-            peer = lax.rem(me + k, n)
+            peer = peer_of(k)
             pltpu.make_async_remote_copy(
                 src_ref=source(peer), dst_ref=target, send_sem=send.at[phase],
                 recv_sem=recv.at[phase], device_id={"sub": peer}, device_id_type=MESH,
             ).start()
             return carry
 
-        lax.fori_loop(1, n, put, 0)
+        lax.fori_loop(0, n - 1, put, 0)
 
     def arrive(phase, whole):
         pltpu.make_async_copy(whole, whole, recv.at[phase]).wait()
@@ -218,20 +251,45 @@
     full_ref[...] = whole
     g_src[...] = mm3(full[col], whole, NT)
 
-    start(5, row_of(g_src), g_dst.at[pl.ds(me, 1), :])
+    group = rows // plane
+    pltpu.make_async_copy(
+        g_src.at[pl.ds(my_part * group, group), :], g_dst.at[my_part], recv.at[5]
+    ).start()
+    for _, dx, core in plane_mates[-(plane - 1) :]:
+        part = lax.rem(my_x + dx, across) * PAIR + lax.rem(my_core + core, PAIR)
+        pltpu.make_async_remote_copy(
+            src_ref=g_src.at[pl.ds(part * group, group), :], dst_ref=g_dst.at[my_part],
+            send_sem=send.at[5], recv_sem=recv.at[5], device_id_type=MESH,
+            device_id={"sub": at(my_x + dx, my_z, my_core + core)},
+        ).start()
     arrive(5, g_dst)
-    h_src[...] = jnp.sum(g_dst[...], axis=0, keepdims=True) / (width * n)
-
-    start(6, lambda r: h_src, gram.at[col, pl.ds(me, 1), :])
-    arrive(6, gram.at[col])
-    start_col(7, gram)
-    arrive(7, gram.at[pl.ds(0, m - 1)])
+    h_src[...] = jnp.sum(g_dst[...], axis=0)
+
+    pltpu.make_async_copy(h_src, h_dst.at[my_z], recv.at[6]).start()
+    for dz in (4, 3, 5, 2, 6, 1, 7):
+        pltpu.make_async_remote_copy(
+            src_ref=h_src, dst_ref=h_dst.at[my_z], send_sem=send.at[6], recv_sem=recv.at[6],
+            device_id={"sub": at(my_x, my_z + dz, my_core)}, device_id_type=MESH,
+        ).start()
+    arrive(6, h_dst)
+    i_src[...] = jnp.sum(h_dst[...], axis=0) / (width * n)
+
+    place = gram.at[col * plane + my_part]
+    pltpu.make_async_copy(i_src, place, recv.at[7]).start()
+    for dy, dx, core in plane_mates:
+        pltpu.make_async_remote_copy(
+            src_ref=i_src, dst_ref=place, send_sem=send.at[7], recv_sem=recv.at[7],
+            device_id={"sub": at(my_x + dx, my_z, my_core + core), "col": lax.rem(col + dy, m)},
+            device_id_type=MESH,
+        ).start()
+    arrive(7, gram)
     gram_ref[...] = gram[...].reshape(m * rows, m * rows)
 
-    for phase, ref in ((0, a_src), (1, b_src), (2, c_src), (3, d_src), (5, g_src), (6, g_dst)):
-        pltpu.make_async_copy(ref, ref, send.at[phase]).wait()
-    for phase, ref in ((4, full), (7, gram)):
-        sent = ref.at[pl.ds(0, m - 1)]
+    for phase, sent in (
+        (0, a_src), (1, b_src), (2, c_src), (3, d_src), (4, full.at[pl.ds(0, m - 1)]),
+        (5, g_dst.at[pl.ds(0, plane - 1)]), (6, h_dst.at[pl.ds(0, RING - 1)]),
+        (7, gram.at[pl.ds(0, m * plane - 1)]),
+    ):
         pltpu.make_async_copy(sent, sent, send.at[phase]).wait()
 
 
@@ -240,6 +298,8 @@
     rows, width = omega.shape
     dofs = flexibility.shape[0]
     order = m * rows
+    plane = n // RING
+    group = rows // plane
     vmem = pl.BlockSpec(memory_space=pltpu.VMEM)
     return pl.pallas_call(
         functools.partial(sketch_kernel, n, m),
@@ -261,9 +321,11 @@
             pltpu.VMEM((n, width), F32),
             pltpu.VMEM((m, rows, width), F32),
             pltpu.VMEM((rows, order), F32),
-            pltpu.VMEM((n, order), F32),
-            pltpu.VMEM((1, order), F32),
-            pltpu.VMEM((m, rows, order), F32),
+            pltpu.VMEM((plane, group, order), F32),
+            pltpu.VMEM((group, order), F32),
+            pltpu.VMEM((RING, group, order), F32),
+            pltpu.VMEM((group, order), F32),
+            pltpu.VMEM((m * plane, group, order), F32),
             pltpu.SemaphoreType.DMA,
             pltpu.SemaphoreType.DMA((8,)),
             pltpu.SemaphoreType.DMA((8,)),

time: 118 us -> 112 us (0.949)
  Pallas kernels: 117 us -> 111 us
    pallas_call x1, Pallas kernels: 69.3 us -> 63.8 us  [sketch_and_gram(): pl.pallas_call(functools.partial(sketch_kernel, n, m), out_shape=(jax.Sha...]
where the time goes in v3:
time: 112 us
  Pallas kernels  111 us (99%)
    pallas_call x1, Pallas kernels, sketch_and_gram(): pl.pallas_call(functools.partial(sketch_kernel, n, m), out_shape=(jax.Sha...  63.8 us
    pallas_call x1, Pallas kernels, finish(): pl.pallas_call(finish_kernel, out_shape=(jax.ShapeDtypeStruct((rows, widt...  47.4 us

profile of v3, /device:TPU:1, one launch (start us, length us, event | category | flops | bytes accessed | tf_op | source)
XLA Modules:
  0.0 111.9 jit_solution(16955599954289022042)
XLA Ops:
  0.6 63.8 %sketch_and_gram.1 = (f32[256,384]{1,0:T(8,128)}, f32[256,256]{1,0:T(8,128)}) custom-call(bf16[64,384]{1,0:T(8,128)(2,1)} %omega_ref.1, bf16[768,768]{1,0:T(8,128)(2,1)} %bitcast.3, s32[6,64]{1,0:T(8,128)} %bitcast.4, s32[6,64]{1,0:T(8,128)} %bitcast.5), custom_call_target="tpu_custom_call" | custom-call | tf_op jit(solution)/shard_map/sketch_and_gram/pallas_call | solution.py:304
  64.5 47.4 %factor_and_basis.1 = (f32[64,384]{1,0:T(8,128)}, f32[64,384]{1,0:T(8,128)}, f32[256,256]{1,0:T(8,128)}) custom-call(f32[256,384]{1,0:T(8,128)} %get-tuple-element.5.full_ref, f32[256,256]{1,0:T(8,128)} %get-tuple-element.6.gram_ref), custom_call_target="tpu_custom_call" | custom-call | tf_op jit(solution)/shard_map/factor_and_basis/pallas_call | solution.py:90

commit v4 on v3

--- a/solution.py
+++ b/solution.py
@@ -97,6 +97,7 @@
         in_specs=[pl.BlockSpec(memory_space=pltpu.VMEM)] * 2,
         out_specs=(pl.BlockSpec(memory_space=pltpu.VMEM),) * 3,
         scratch_shapes=[pltpu.VMEM((order, order), F32)] * 2,
+        compiler_params=pltpu.CompilerParams(vmem_limit_bytes=12 << 20),
         name="factor_and_basis",
     )(full, gram)
 
@@ -122,8 +123,8 @@
 
 
 def sketch_kernel(
-    n, m, omega_ref, flex_ref, row_ref, sign_ref, full_ref, gram_ref,
-    spare, flex, a_src, a_dst, b_src, b_dst, c_src, c_dst, d_src, full, g_src, g_dst, h_src, h_dst, i_src, gram,
+    n, m, omega_hbm, flex_ref, row_hbm, sign_hbm, full_ref, gram_ref,
+    omega_ref, row_ref, sign_ref, load_sem, spare, flex, a_src, a_dst, b_src, b_dst, c_src, c_dst, d_src, full, g_src, g_dst, h_src, h_dst, i_src, gram,
     flex_sem, send, recv,
 ):
     me = lax.axis_index("sub")
@@ -133,9 +134,6 @@
     length = b_src.shape[1] // refs
     owned = width // length
 
-    load = pltpu.make_async_copy(flex_ref, flex, flex_sem)
-    load.start()
-
     across = n // (RING * PAIR)
     plane = across * PAIR
     my_x = lax.div(me, RING * PAIR)
@@ -175,6 +173,15 @@
             barrier, inc=1, device_id_type=MESH,
             device_id={"sub": at(my_x + dx, my_z, my_core + core), "col": lax.rem(col + dy, m)},
         )
+    tables = [
+        pltpu.make_async_copy(row_hbm, row_ref, load_sem.at[1]),
+        pltpu.make_async_copy(sign_hbm, sign_ref, load_sem.at[2]),
+    ]
+    load = pltpu.make_async_copy(flex_ref, flex, flex_sem)
+    first = pltpu.make_async_copy(omega_hbm, omega_ref, load_sem.at[0])
+    for copy in [first, *tables, load]:
+        copy.start()
+    first.wait()
     a_src[...] = omega_ref[...].astype(F32)
     pl.semaphore_wait(barrier, n - 1 + len(others))
 
@@ -210,6 +217,8 @@
         return lambda r: ref.at[pl.ds(r, 1), :]
 
     start(0, row_of(a_src), a_dst.at[pl.ds(me, 1), :])
+    for copy in tables:
+        copy.wait()
     spot = lax.broadcasted_iota(jnp.int32, (owned * n, n), 0)
     piece = sum([jnp.where(spot >= n * j, 1, 0) for j in range(1, owned)])
     named = owned * (spot - n * piece) + piece
@@ -307,9 +316,13 @@
             jax.ShapeDtypeStruct((order, width), F32),
             jax.ShapeDtypeStruct((order, order), F32),
         ),
-        in_specs=[vmem, pl.BlockSpec(memory_space=pl.ANY), vmem, vmem],
+        in_specs=[pl.BlockSpec(memory_space=pltpu.HBM)] * 4,
         out_specs=(vmem, vmem),
         scratch_shapes=[
+            pltpu.VMEM(omega.shape, omega.dtype),
+            pltpu.VMEM(block_row.shape[::-1], jnp.int32),
+            pltpu.VMEM(block_row.shape[::-1], jnp.int32),
+            pltpu.SemaphoreType.DMA((3,)),
             pltpu.VMEM((8, 1, dofs), F32),
             pltpu.VMEM((dofs, dofs), BF16),
             pltpu.VMEM((rows, width), F32),
@@ -330,7 +343,9 @@
             pltpu.SemaphoreType.DMA((8,)),
             pltpu.SemaphoreType.DMA((8,)),
         ],
-        compiler_params=pltpu.CompilerParams(collective_id=0, has_side_effects=True),
+        compiler_params=pltpu.CompilerParams(
+            collective_id=0, has_side_effects=True, vmem_limit_bytes=12 << 20
+        ),
         name="sketch_and_gram",
     )(omega, flexibility, block_row.T, block_sign.T)
 

time: 112 us -> 112 us (level)
  local copies, waits for them, and re-layouts: 0 us -> 3.43 us
  Pallas kernels: 111 us -> 108 us
    unnamed x0 -> x8, local copies, waits for them, and re-layouts: none -> 3.43 us
    pallas_call x1, Pallas kernels: 63.8 us -> 62 us  [sketch_and_gram(): pl.pallas_call(functools.partial(sketch_kernel, n, m), out_shape=(jax.Sha...]
    pallas_call x1, Pallas kernels: 47.4 us -> 46.2 us  [finish(): pl.pallas_call(finish_kernel, out_shape=(jax.ShapeDtypeStruct((rows, widt...]
where the time goes in v4:
time: 112 us
  Pallas kernels  108 us (96%)
  local copies, waits for them, and re-layouts  3.43 us (3%)
    pallas_call x1, Pallas kernels, sketch_and_gram(): pl.pallas_call(functools.partial(sketch_kernel, n, m), out_shape=(jax.Sha...  62 us
    pallas_call x1, Pallas kernels, finish(): pl.pallas_call(finish_kernel, out_shape=(jax.ShapeDtypeStruct((rows, widt...  46.2 us
    unnamed x8, local copies, waits for them, and re-layouts  3.43 us

profile of v4, /device:TPU:1, one launch (start us, length us, event | category | flops | bytes accessed | tf_op | source)
XLA Modules:
  0.0 112.2 jit_solution(6980293015181937041)
XLA Ops:
  0.6 0.0 copy-start
  0.6 1.3 %copy-done = bf16[1,768,768]{2,1,0:T(8,128)(2,1)S(1)} copy-done((bf16[1,768,768]{2,1,0:T(8,128)(2,1)S(1)}, bf16[1,768,768]{2,1,0:T(8,128)(2,1)}, u32[]{:S(2)}) %copy-start) | copy-done | bytes 1179672
  1.9 0.0 copy-start.1
  1.9 0.8 copy-done.1
  2.7 0.0 copy-start.2
  2.7 0.7 copy-done.2
  3.4 0.0 copy-start.3
  3.4 0.7 copy-done.3
  4.1 62.0 %sketch_and_gram.1 = (f32[256,384]{1,0:T(8,128)S(1)}, f32[256,256]{1,0:T(8,128)S(1)}) custom-call(bf16[64,384]{1,0:T(8,128)(2,1)S(1)} %copy-done.1, bf16[768,768]{1,0:T(8,128)(2,1)S(1)} %bitcast.3, s32[6,64]{1,0:T(8,128)S(1)} %bitcast.4, s32[6,64]{1,0:T(8,128)S(1)} %bitcast.5), custom_call_target="tpu_custom_call" | custom-call | tf_op jit(solution)/shard_map/sketch_and_gram/pallas_call | solution.py:313
  66.1 46.2 %factor_and_basis.1 = (f32[64,384]{1,0:T(8,128)}, f32[64,384]{1,0:T(8,128)}, f32[256,256]{1,0:T(8,128)}) custom-call(f32[256,384]{1,0:T(8,128)S(1)} %get-tuple-element.5.full_ref, f32[256,256]{1,0:T(8,128)S(1)} %get-tuple-element.6.gram_ref), custom_call_target="tpu_custom_call" | custom-call | tf_op jit(solution)/shard_map/factor_and_basis/pallas_call | solution.py:90
Async XLA Ops:
  0.6 1.3 %copy-start = (bf16[1,768,768]{2,1,0:T(8,128)(2,1)S(1)}, bf16[1,768,768]{2,1,0:T(8,128)(2,1)}, u32[]{:S(2)}) copy-start(bf16[1,768,768]{2,1,0:T(8,128)(2,1)} %param.4) | copy-start | bytes 3538948
  1.9 0.8 copy-start.1
  2.7 0.7 copy-start.2
  3.4 0.7 copy-start.3

commit v5 on v4

--- a/solution.py
+++ b/solution.py
@@ -347,7 +347,7 @@
             collective_id=0, has_side_effects=True, vmem_limit_bytes=12 << 20
         ),
         name="sketch_and_gram",
-    )(omega, flexibility, block_row.T, block_sign.T)
+    )(*(pltpu.with_memory_space_constraint(x, pltpu.HBM) for x in (omega, flexibility, block_row.T, block_sign.T)))
 
 
 def shards(flexibility, omega, block_row, block_sign):

time: 112 us -> 110 us (0.982)
  local copies, waits for them, and re-layouts: 3.43 us -> 0 us
    unnamed x8 -> x0, local copies, waits for them, and re-layouts: 3.43 us -> none
where the time goes in v5:
time: 110 us; the launch traced here: 109 us
  Pallas kernels  109 us (99%)
    pallas_call x1, Pallas kernels, sketch_and_gram(): pl.pallas_call(functools.partial(sketch_kernel, n, m), out_shape=(jax.Sha...  62.7 us
    pallas_call x1, Pallas kernels, finish(): pl.pallas_call(finish_kernel, out_shape=(jax.ShapeDtypeStruct((rows, widt...  46.2 us

profile of v5, /device:TPU:1, one launch (start us, length us, event | category | flops | bytes accessed | tf_op | source)
XLA Modules:
  0.0 109.5 jit_solution(2064820559435174201)
XLA Ops:
  0.6 62.7 %sketch_and_gram.1 = (f32[256,384]{1,0:T(8,128)S(1)}, f32[256,256]{1,0:T(8,128)S(1)}) custom-call(bf16[64,384]{1,0:T(8,128)(2,1)} %omega_hbm.1, bf16[768,768]{1,0:T(8,128)(2,1)} %bitcast.3, s32[6,64]{1,0:T(8,128)} %bitcast.4, s32[6,64]{1,0:T(8,128)} %bitcast.5), custom_call_target="tpu_custom_call" | custom-call | tf_op jit(solution)/shard_map/sketch_and_gram/pallas_call | solution.py:313
  63.3 46.2 %factor_and_basis.1 = (f32[64,384]{1,0:T(8,128)}, f32[64,384]{1,0:T(8,128)}, f32[256,256]{1,0:T(8,128)}) custom-call(f32[256,384]{1,0:T(8,128)S(1)} %get-tuple-element.5.full_ref, f32[256,256]{1,0:T(8,128)S(1)} %get-tuple-element.6.gram_ref), custom_call_target="tpu_custom_call" | custom-call | tf_op jit(solution)/shard_map/factor_and_basis/pallas_call | solution.py:90

commit v6 on v5

--- a/solution.py
+++ b/solution.py
@@ -145,12 +145,27 @@
         x, z, core = lax.rem(x, across), lax.rem(z, RING), lax.rem(core, PAIR)
         return (x * RING + z) * PAIR + core
 
-    def peer_of(k):
+    def offset_of(k):
         in_plane = lax.rem(k, plane)
         dz = centre_out(lax.div(k, plane), RING)
         dx = centre_out(lax.div(in_plane, PAIR), across)
-        return at(my_x + dx, my_z + dz, my_core + 1 - lax.rem(in_plane, PAIR))
-
+        return dx, dz, 1 - lax.rem(in_plane, PAIR)
+
+    def ahead(k):
+        dx, dz, core = offset_of(k)
+        return at(my_x + dx, my_z + dz, my_core + core)
+
+    def behind(k):
+        dx, dz, core = offset_of(k)
+        return at(my_x + across - dx, my_z + RING - dz, my_core + core)
+
+    def row_of(device):
+        x = lax.div(device, RING * PAIR)
+        z = lax.rem(lax.div(device, PAIR), RING)
+        return z * plane + x * PAIR + lax.rem(device, PAIR)
+
+    my_row = row_of(me)
+    far = 3 * plane
     plane_mates = [
         (dy, dx, core)
         for dy in (2, 1, 3, 0)
@@ -162,7 +177,7 @@
 
     def greet(k, carry):
         pl.semaphore_signal(
-            barrier, inc=1, device_id={"sub": peer_of(k)}, device_id_type=MESH
+            barrier, inc=1, device_id={"sub": ahead(k)}, device_id_type=MESH
         )
         return carry
 
@@ -185,38 +200,34 @@
     a_src[...] = omega_ref[...].astype(F32)
     pl.semaphore_wait(barrier, n - 1 + len(others))
 
-    def start(phase, source, target):
-        own = pltpu.make_async_copy(source(me), target, recv.at[phase])
-        own.start()
-        pltpu.make_async_copy(
-            source(me), spare.at[phase, :, pl.ds(0, target.shape[1])], send.at[phase]
-        ).start()
-
+    def send_rows(phase, arrival, span, peer_of, source, target):
         def put(k, carry):
             peer = peer_of(k)
             pltpu.make_async_remote_copy(
-                src_ref=source(peer), dst_ref=target, send_sem=send.at[phase],
-                recv_sem=recv.at[phase], device_id={"sub": peer}, device_id_type=MESH,
+                src_ref=source(k, peer), dst_ref=target(k), send_sem=send.at[phase],
+                recv_sem=recv.at[arrival], device_id={"sub": peer}, device_id_type=MESH,
             ).start()
             return carry
 
-        lax.fori_loop(0, n - 1, put, 0)
+        lax.fori_loop(*span, put, 0)
+
+    def keep_row(phase, arrival, source, target):
+        pltpu.make_async_copy(source, target, recv.at[arrival]).start()
+        pltpu.make_async_copy(
+            source, spare.at[phase, :, pl.ds(0, source.shape[1])], send.at[phase]
+        ).start()
 
     def arrive(phase, whole):
         pltpu.make_async_copy(whole, whole, recv.at[phase]).wait()
 
-    def start_col(phase, ref):
-        for k in range(1, m):
-            pltpu.make_async_remote_copy(
-                src_ref=ref.at[col], dst_ref=ref.at[col], send_sem=send.at[phase],
-                recv_sem=recv.at[phase], device_id={"col": lax.rem(col + k, m)},
-                device_id_type=MESH,
-            ).start()
-
-    def row_of(ref):
-        return lambda r: ref.at[pl.ds(r, 1), :]
-
-    start(0, row_of(a_src), a_dst.at[pl.ds(me, 1), :])
+    def row(ref, r):
+        return ref.at[pl.ds(r, 1), :]
+
+    send_rows(
+        0, 0, (0, n - 1), ahead, lambda k, peer: row(a_src, row_of(peer)),
+        lambda k: row(a_dst, me),
+    )
+    keep_row(0, 0, row(a_src, my_row), row(a_dst, me))
     for copy in tables:
         copy.wait()
     spot = lax.broadcasted_iota(jnp.int32, (owned * n, n), 0)
@@ -235,14 +246,21 @@
     )
     b_src[...] = spread_rows(wanted, refs)
 
-    start(1, row_of(b_src), b_dst.at[pl.ds(me, 1), :])
+    for arrival, span in ((1, (0, far)), (8, (far, n - 1))):
+        send_rows(
+            1, arrival, span, ahead, lambda k, peer: row(b_src, peer), lambda k: row(b_dst, k)
+        )
+    keep_row(1, 8, row(b_src, me), row(b_dst, n - 1))
     load.wait()
-    arrive(1, b_dst)
-    c_src[...] = lax.dot_general(
-        b_dst[...].astype(BF16), flex[...], NT, preferred_element_type=F32
-    )
-
-    start(2, row_of(c_src), c_dst.at[pl.ds(me, 1), :])
+    for arrival, low, high, last in ((8, far, n, n - 1), (1, 0, far, far)):
+        arrive(arrival, b_dst.at[pl.ds(low, high - low), :])
+        c_src[low:high, :] = lax.dot_general(
+            b_dst[low:high, :].astype(BF16), flex[...], NT, preferred_element_type=F32
+        )
+        send_rows(
+            2, 2, (low, last), behind, lambda k, peer: row(c_src, k), lambda k: row(c_dst, me)
+        )
+    keep_row(2, 2, row(c_src, n - 1), row(c_dst, me))
     arrive(2, c_dst)
     terms = stack_lanes(c_dst[...], length)
     high, rest = halves(terms)
@@ -252,9 +270,22 @@
     )
     d_src[...] = spread_rows(total, owned)
 
-    start(3, row_of(d_src), full.at[col, pl.ds(me, 1), :])
-    arrive(3, full.at[col])
-    start_col(4, full)
+    mine = full.at[col]
+    for arrival, span in ((3, (0, far)), (9, (far, n - 1))):
+        send_rows(
+            3, arrival, span, ahead, lambda k, peer: row(d_src, peer), lambda k: row(mine, my_row)
+        )
+    keep_row(3, 9, row(d_src, me), row(mine, my_row))
+    for arrival, count, group_dz in ((9, n - far, (0, 1, 7, 2, 6)), (3, far, (3, 5, 4))):
+        arrive(arrival, mine.at[pl.ds(0, count), :])
+        for dz in group_dz:
+            z = lax.rem(my_z + dz, RING)
+            part = mine.at[pl.ds(pl.multiple_of(z * plane, plane), plane), :]
+            for dy in (2, 1, 3):
+                pltpu.make_async_remote_copy(
+                    src_ref=part, dst_ref=part, send_sem=send.at[4], recv_sem=recv.at[4],
+                    device_id={"col": lax.rem(col + dy, m)}, device_id_type=MESH,
+                ).start()
     arrive(4, full.at[pl.ds(0, m - 1)])
     whole = full[...].reshape(m * rows, width)
     full_ref[...] = whole
@@ -341,7 +372,7 @@
             pltpu.VMEM((m * plane, group, order), F32),
             pltpu.SemaphoreType.DMA,
             pltpu.SemaphoreType.DMA((8,)),
-            pltpu.SemaphoreType.DMA((8,)),
+            pltpu.SemaphoreType.DMA((10,)),
         ],
         compiler_params=pltpu.CompilerParams(
             collective_id=0, has_side_effects=True, vmem_limit_bytes=12 << 20

time: 110 us -> 110 us (level)
  no operation moved by 1% of the time
where the time goes in v6:
time: 110 us
  Pallas kernels  110 us (100%)
    pallas_call x1, Pallas kernels, sketch_and_gram(): pl.pallas_call(functools.partial(sketch_kernel, n, m), out_shape=(jax.Sha...  63.3 us
    pallas_call x1, Pallas kernels, finish(): pl.pallas_call(finish_kernel, out_shape=(jax.ShapeDtypeStruct((rows, widt...  46.2 us

profile of v6, /device:TPU:1, one launch (start us, length us, event | category | flops | bytes accessed | tf_op | source)
XLA Modules:
  0.0 110.2 jit_solution(12870547736835723787)
XLA Ops:
  0.6 63.3 %sketch_and_gram.1 = (f32[256,384]{1,0:T(8,128)S(1)}, f32[256,256]{1,0:T(8,128)S(1)}) custom-call(bf16[64,384]{1,0:T(8,128)(2,1)} %omega_hbm.1, bf16[768,768]{1,0:T(8,128)(2,1)} %bitcast.3, s32[6,64]{1,0:T(8,128)} %bitcast.4, s32[6,64]{1,0:T(8,128)} %bitcast.5), custom_call_target="tpu_custom_call" | custom-call | tf_op jit(solution)/shard_map/sketch_and_gram/pallas_call | solution.py:344
  64.0 46.2 %factor_and_basis.1 = (f32[64,384]{1,0:T(8,128)}, f32[64,384]{1,0:T(8,128)}, f32[256,256]{1,0:T(8,128)}) custom-call(f32[256,384]{1,0:T(8,128)S(1)} %get-tuple-element.5.full_ref, f32[256,256]{1,0:T(8,128)S(1)} %get-tuple-element.6.gram_ref), custom_call_target="tpu_custom_call" | custom-call | tf_op jit(solution)/shard_map/factor_and_basis/pallas_call | solution.py:90

commit v7 on v5

--- a/solution.py
+++ b/solution.py
@@ -105,6 +105,7 @@
 MESH = pl.DeviceIdType.MESH
 RING = 8
 PAIR = 2
+SEATS = 8
 TN = (((0,), (0,)), ((), ()))
 
 
@@ -124,14 +125,14 @@
 
 def sketch_kernel(
     n, m, omega_hbm, flex_ref, row_hbm, sign_hbm, full_ref, gram_ref,
-    omega_ref, row_ref, sign_ref, load_sem, spare, flex, a_src, a_dst, b_src, b_dst, c_src, c_dst, d_src, full, g_src, g_dst, h_src, h_dst, i_src, gram,
+    omega_ref, row_ref, sign_ref, load_sem, spare, spare_half, flex, a_src, a_dst, b_src, b_dst, c_src, c_dst, d_src, full, g_src, g_dst, h_src, h_dst, i_src, gram,
     flex_sem, send, recv,
 ):
     me = lax.axis_index("sub")
     col = lax.axis_index("col")
     rows, width = a_src.shape
     refs = row_ref.shape[0]
-    length = b_src.shape[1] // refs
+    length = c_src.shape[1] // refs
     owned = width // length
 
     across = n // (RING * PAIR)
@@ -185,11 +186,13 @@
     a_src[...] = omega_ref[...].astype(F32)
     pl.semaphore_wait(barrier, n - 1 + len(others))
 
-    def start(phase, source, target):
+    def start(phase, source, target, unread=None):
         own = pltpu.make_async_copy(source(me), target, recv.at[phase])
         own.start()
         pltpu.make_async_copy(
-            source(me), spare.at[phase, :, pl.ds(0, target.shape[1])], send.at[phase]
+            source(me),
+            spare.at[phase, :, pl.ds(0, target.shape[1])] if unread is None else unread,
+            send.at[phase],
         ).start()
 
         def put(k, carry):
@@ -229,17 +232,27 @@
         ],
         axis=1,
     ).astype(BF16)
+    held = lax.broadcasted_iota(jnp.int32, (refs * n, SEATS * n), 0)
+    block = sum([jnp.where(held >= n * l, 1, 0) for l in range(1, refs)])
+    seat = SEATS * (held - n * block) + block
+    seat = jnp.where(lax.broadcasted_iota(jnp.int32, seat.shape, 1) == seat, 1.0, 0.0)
+    seat = seat.astype(F32).astype(BF16)
+    seated = lax.dot_general(pick, seat, NN, preferred_element_type=F32).astype(BF16)
     arrive(0, a_dst)
     wanted = lax.dot_general(
-        pick, stack_lanes(a_dst[...], length).astype(BF16), TN, preferred_element_type=F32
+        seated, stack_lanes(a_dst[...], length).astype(BF16), TN, preferred_element_type=F32
     )
-    b_src[...] = spread_rows(wanted, refs)
-
-    start(1, row_of(b_src), b_dst.at[pl.ds(me, 1), :])
+    b_src[...] = wanted.astype(BF16)
+
+    def seats_of(ref):
+        return lambda r: ref.at[pl.ds(pl.multiple_of(r * SEATS, SEATS), SEATS), :]
+
+    start(1, seats_of(b_src), seats_of(b_dst)(me), spare_half)
     load.wait()
     arrive(1, b_dst)
+    signed = lax.dot_general(seat, b_dst[...], NN, preferred_element_type=F32)
     c_src[...] = lax.dot_general(
-        b_dst[...].astype(BF16), flex[...], NT, preferred_element_type=F32
+        spread_rows(signed.astype(BF16), refs), flex[...], NT, preferred_element_type=F32
     )
 
     start(2, row_of(c_src), c_dst.at[pl.ds(me, 1), :])
@@ -306,6 +319,7 @@
     n, m = lax.axis_size("sub"), lax.axis_size("col")
     rows, width = omega.shape
     dofs = flexibility.shape[0]
+    length = dofs // block_row.shape[1]
     order = m * rows
     plane = n // RING
     group = rows // plane
@@ -324,11 +338,12 @@
             pltpu.VMEM(block_row.shape[::-1], jnp.int32),
             pltpu.SemaphoreType.DMA((3,)),
             pltpu.VMEM((8, 1, dofs), F32),
+            pltpu.VMEM((SEATS, length), BF16),
             pltpu.VMEM((dofs, dofs), BF16),
             pltpu.VMEM((rows, width), F32),
             pltpu.VMEM((n, width), F32),
-            pltpu.VMEM((n, dofs), F32),
-            pltpu.VMEM((rows, dofs), F32),
+            pltpu.VMEM((n * SEATS, length), BF16),
+            pltpu.VMEM((n * SEATS, length), BF16),
             pltpu.VMEM((rows, dofs), F32),
             pltpu.VMEM((n, dofs), F32),
             pltpu.VMEM((n, width), F32),

time: 110 us -> 109 us (level)
  no operation moved by 1% of the time
where the time goes in v7:
time: 109 us
  Pallas kernels  108 us (99%)
    pallas_call x1, Pallas kernels, sketch_and_gram(): pl.pallas_call(functools.partial(sketch_kernel, n, m), out_shape=(jax.Sha...  61.9 us
    pallas_call x1, Pallas kernels, finish(): pl.pallas_call(finish_kernel, out_shape=(jax.ShapeDtypeStruct((rows, widt...  46.2 us

profile of v7, /device:TPU:1, one launch (start us, length us, event | category | flops | bytes accessed | tf_op | source)
XLA Modules:
  0.0 108.7 jit_solution(12742566959988785867)
XLA Ops:
  0.6 61.9 %sketch_and_gram.1 = (f32[256,384]{1,0:T(8,128)S(1)}, f32[256,256]{1,0:T(8,128)S(1)}) custom-call(bf16[64,384]{1,0:T(8,128)(2,1)} %omega_hbm.1, bf16[768,768]{1,0:T(8,128)(2,1)} %bitcast.3, s32[6,64]{1,0:T(8,128)} %bitcast.4, s32[6,64]{1,0:T(8,128)} %bitcast.5), custom_call_target="tpu_custom_call" | custom-call | tf_op jit(solution)/shard_map/sketch_and_gram/pallas_call | solution.py:327
  62.5 46.2 %factor_and_basis.1 = (f32[64,384]{1,0:T(8,128)}, f32[64,384]{1,0:T(8,128)}, f32[256,256]{1,0:T(8,128)}) custom-call(f32[256,384]{1,0:T(8,128)S(1)} %get-tuple-element.5.full_ref, f32[256,256]{1,0:T(8,128)S(1)} %get-tuple-element.6.gram_ref), custom_call_target="tpu_custom_call" | custom-call | tf_op jit(solution)/shard_map/factor_and_basis/pallas_call | solution.py:90

commit v8 on v7

--- a/solution.py
+++ b/solution.py
@@ -52,9 +52,10 @@
     z = err + n + mm3(n, err)
     resid = z + n.T + mm3(z, n, NT)
     p = resid * phi_mask
-    n = n - p - mm1(p, n)
+    change = p + mm1(p, n)
     miss = jnp.sum(resid * resid)
-    z = err + n + mm3(n, err)
+    n = n - change
+    z = z - change - mm1(change, err)
     upper_ref[...] = jnp.where(i_row <= i_col, (eye + z) * (d_row * s_row), 0.0)
     lower[...] = jnp.where(i_row >= i_col, (eye + n) * s_row, 0.0)
 
@@ -119,8 +120,8 @@
 
 
 def centre_out(i, size):
-    half = lax.div(i + 1, 2)
-    return size // 2 + half * (1 - 2 * lax.rem(i, 2))
+    half = (i + 1) // 2
+    return size // 2 + half * (1 - 2 * (i % 2))
 
 
 def sketch_kernel(
@@ -147,10 +148,10 @@
         return (x * RING + z) * PAIR + core
 
     def peer_of(k):
-        in_plane = lax.rem(k, plane)
-        dz = centre_out(lax.div(k, plane), RING)
-        dx = centre_out(lax.div(in_plane, PAIR), across)
-        return at(my_x + dx, my_z + dz, my_core + 1 - lax.rem(in_plane, PAIR))
+        in_plane = k % plane
+        dz = centre_out(k // plane, RING)
+        dx = centre_out(in_plane // PAIR, across)
+        return at(my_x + dx, my_z + dz, my_core + 1 - in_plane % PAIR)
 
     plane_mates = [
         (dy, dx, core)
@@ -167,7 +168,8 @@
         )
         return carry
 
-    lax.fori_loop(0, n - 1, greet, 0)
+    for k in range(n - 1):
+        greet(k, 0)
     others = [mate for mate in plane_mates if mate[0]]
     for dy, dx, core in others:
         pl.semaphore_signal(
@@ -187,6 +189,16 @@
     pl.semaphore_wait(barrier, n - 1 + len(others))
 
     def start(phase, source, target, unread=None):
+        def put(k, carry):
+            peer = peer_of(k)
+            pltpu.make_async_remote_copy(
+                src_ref=source(peer), dst_ref=target, send_sem=send.at[phase],
+                recv_sem=recv.at[phase], device_id={"sub": peer}, device_id_type=MESH,
+            ).start()
+            return carry
+
+        for k in range(n - 1):
+            put(k, 0)
         own = pltpu.make_async_copy(source(me), target, recv.at[phase])
         own.start()
         pltpu.make_async_copy(
@@ -194,16 +206,6 @@
             spare.at[phase, :, pl.ds(0, target.shape[1])] if unread is None else unread,
             send.at[phase],
         ).start()
-
-        def put(k, carry):
-            peer = peer_of(k)
-            pltpu.make_async_remote_copy(
-                src_ref=source(peer), dst_ref=target, send_sem=send.at[phase],
-                recv_sem=recv.at[phase], device_id={"sub": peer}, device_id_type=MESH,
-            ).start()
-            return carry
-
-        lax.fori_loop(0, n - 1, put, 0)
 
     def arrive(phase, whole):
         pltpu.make_async_copy(whole, whole, recv.at[phase]).wait()
@@ -274,9 +276,6 @@
     g_src[...] = mm3(full[col], whole, NT)
 
     group = rows // plane
-    pltpu.make_async_copy(
-        g_src.at[pl.ds(my_part * group, group), :], g_dst.at[my_part], recv.at[5]
-    ).start()
     for _, dx, core in plane_mates[-(plane - 1) :]:
         part = lax.rem(my_x + dx, across) * PAIR + lax.rem(my_core + core, PAIR)
         pltpu.make_async_remote_copy(
@@ -284,26 +283,29 @@
             send_sem=send.at[5], recv_sem=recv.at[5], device_id_type=MESH,
             device_id={"sub": at(my_x + dx, my_z, my_core + core)},
         ).start()
+    pltpu.make_async_copy(
+        g_src.at[pl.ds(my_part * group, group), :], g_dst.at[my_part], recv.at[5]
+    ).start()
     arrive(5, g_dst)
     h_src[...] = jnp.sum(g_dst[...], axis=0)
 
-    pltpu.make_async_copy(h_src, h_dst.at[my_z], recv.at[6]).start()
     for dz in (4, 3, 5, 2, 6, 1, 7):
         pltpu.make_async_remote_copy(
             src_ref=h_src, dst_ref=h_dst.at[my_z], send_sem=send.at[6], recv_sem=recv.at[6],
             device_id={"sub": at(my_x, my_z + dz, my_core)}, device_id_type=MESH,
         ).start()
+    pltpu.make_async_copy(h_src, h_dst.at[my_z], recv.at[6]).start()
     arrive(6, h_dst)
     i_src[...] = jnp.sum(h_dst[...], axis=0) / (width * n)
 
     place = gram.at[col * plane + my_part]
-    pltpu.make_async_copy(i_src, place, recv.at[7]).start()
     for dy, dx, core in plane_mates:
         pltpu.make_async_remote_copy(
             src_ref=i_src, dst_ref=place, send_sem=send.at[7], recv_sem=recv.at[7],
             device_id={"sub": at(my_x + dx, my_z, my_core + core), "col": lax.rem(col + dy, m)},
             device_id_type=MESH,
         ).start()
+    pltpu.make_async_copy(i_src, place, recv.at[7]).start()
     arrive(7, gram)
     gram_ref[...] = gram[...].reshape(m * rows, m * rows)
 

time: 109 us -> 106 us (0.972)
  Pallas kernels: 108 us -> 105 us
    pallas_call x1, Pallas kernels: 61.9 us -> 59.4 us  [sketch_and_gram(): pl.pallas_call(functools.partial(sketch_kernel, n, m), out_shape=(jax.Sha...]
where the time goes in v8:
time: 106 us
  Pallas kernels  105 us (99%)
    pallas_call x1, Pallas kernels, sketch_and_gram(): pl.pallas_call(functools.partial(sketch_kernel, n, m), out_shape=(jax.Sha...  59.4 us
    pallas_call x1, Pallas kernels, finish(): pl.pallas_call(finish_kernel, out_shape=(jax.ShapeDtypeStruct((rows, widt...  46 us

profile of v8, /device:TPU:1, one launch (start us, length us, event | category | flops | bytes accessed | tf_op | source)
XLA Modules:
  0.0 106.0 jit_solution(1171150220727273127)
XLA Ops:
  0.6 59.4 %sketch_and_gram.1 = (f32[256,384]{1,0:T(8,128)S(1)}, f32[256,256]{1,0:T(8,128)S(1)}) custom-call(bf16[64,384]{1,0:T(8,128)(2,1)} %omega_hbm.1, bf16[768,768]{1,0:T(8,128)(2,1)} %bitcast.3, s32[6,64]{1,0:T(8,128)} %bitcast.4, s32[6,64]{1,0:T(8,128)} %bitcast.5), custom_call_target="tpu_custom_call" | custom-call | tf_op jit(solution)/shard_map/sketch_and_gram/pallas_call | solution.py:329
  60.0 46.0 %factor_and_basis.1 = (f32[64,384]{1,0:T(8,128)}, f32[64,384]{1,0:T(8,128)}, f32[256,256]{1,0:T(8,128)}) custom-call(f32[256,384]{1,0:T(8,128)S(1)} %get-tuple-element.5.full_ref, f32[256,256]{1,0:T(8,128)S(1)} %get-tuple-element.6.gram_ref), custom_call_target="tpu_custom_call" | custom-call | tf_op jit(solution)/shard_map/factor_and_basis/pallas_call | solution.py:91

commit v9 on v8

--- a/solution.py
+++ b/solution.py
@@ -211,7 +211,7 @@
         pltpu.make_async_copy(whole, whole, recv.at[phase]).wait()
 
     def start_col(phase, ref):
-        for k in range(1, m):
+        for k in sorted(range(1, m), key=lambda step: abs(step - m // 2)):
             pltpu.make_async_remote_copy(
                 src_ref=ref.at[col], dst_ref=ref.at[col], send_sem=send.at[phase],
                 recv_sem=recv.at[phase], device_id={"col": lax.rem(col + k, m)},

time: 106 us -> 106 us (level)
  no operation moved by 1% of the time
where the time goes in v9:
time: 106 us
  Pallas kernels  105 us (99%)
    pallas_call x1, Pallas kernels, sketch_and_gram(): pl.pallas_call(functools.partial(sketch_kernel, n, m), out_shape=(jax.Sha...  59.2 us
    pallas_call x1, Pallas kernels, finish(): pl.pallas_call(finish_kernel, out_shape=(jax.ShapeDtypeStruct((rows, widt...  46 us

profile of v9, /device:TPU:1, one launch (start us, length us, event | category | flops | bytes accessed | tf_op | source)
XLA Modules:
  0.0 105.8 jit_solution(16175923381210889535)
XLA Ops:
  0.6 59.2 %sketch_and_gram.1 = (f32[256,384]{1,0:T(8,128)S(1)}, f32[256,256]{1,0:T(8,128)S(1)}) custom-call(bf16[64,384]{1,0:T(8,128)(2,1)} %omega_hbm.1, bf16[768,768]{1,0:T(8,128)(2,1)} %bitcast.3, s32[6,64]{1,0:T(8,128)} %bitcast.4, s32[6,64]{1,0:T(8,128)} %bitcast.5), custom_call_target="tpu_custom_call" | custom-call | tf_op jit(solution)/shard_map/sketch_and_gram/pallas_call | solution.py:329
  59.8 46.0 %factor_and_basis.1 = (f32[64,384]{1,0:T(8,128)}, f32[64,384]{1,0:T(8,128)}, f32[256,256]{1,0:T(8,128)}) custom-call(f32[256,384]{1,0:T(8,128)S(1)} %get-tuple-element.5.full_ref, f32[256,256]{1,0:T(8,128)S(1)} %get-tuple-element.6.gram_ref), custom_call_target="tpu_custom_call" | custom-call | tf_op jit(solution)/shard_map/factor_and_basis/pallas_call | solution.py:91
